TPU v7x, 128 devices: a whole 4x4x4 slice. The times are simulated.
128 devices in a mesh: pb: 16 (over y, x_hi, core), ka: 8 (over z, x_lo).
Axes of the slice: x: 4 (x_hi: 2, x_lo: 2; x = x_hi * 2 + x_lo), y: 4, z: 4, core: 2. Of those that a mesh axis runs over, the one named last changes fastest.
Arguments:
- bin_states: bfloat16 [8192, 1536], P(('pb', 'ka')), may hold values from -50 to 50
- contacts: int32 [8192, 16384], P('pb', 'ka'), may hold values from 0 to 2047, as said below
- w_query: bfloat16 [1536, 256], replicated, may hold values from -0.15625 to 0.15625
- w_keyval: bfloat16 [1536, 512], replicated, may hold values from -0.15625 to 0.15625
- pair_in: float32 [2, 32], replicated, may hold values from -30 to 30
- pair_shift: float32 [2, 32], replicated, may hold values from -230 to 230
- pair_out: float32 [2, 32], replicated, may hold values from -2.7 to 2.7
- w_out: bfloat16 [256, 1536], replicated, may hold values from -0.375 to 0.375
Outputs:
- mixed_out: bfloat16 [8192, 1536], P(('pb', 'ka'))
Inputs may be any that keep to these rules, and one draw needn't show every extreme that they name: contacts fall off with the distance |c - 8192|; the count at offset zero reaches 2047 in every draw.
All inputs are finite; a program needn't handle non-finite values.
Results may differ from a plain program's by a relative error of at most 0.012.
The roundings to bfloat16 on the way count: a program that leaves them out, or rounds other values in their place, can miss the bound.
Values may be sent and summed in bfloat16 or wider, within the bound.
A program may use at most 128 MiB of HBM per device.

v0:
```python
import jax
import jax.numpy as jnp
from jax import lax
from jax.sharding import PartitionSpec as P

HEADS = 2
HEAD_DIM = 128
PAIR_HIDDEN = 32
HALF_BAND = 8192


def shifted(block, axis, distance):
    devices = range(lax.axis_size(axis))
    route = [((i - distance) % len(devices), i) for i in devices]
    return lax.ppermute(block, axis, route)


def shear_rows(tile):
    leading, height, length = tile.shape
    padded = jnp.pad(tile, ((0, 0), (0, 0), (0, height + 1)))
    flattened = padded.reshape(leading, height * (length + height + 1))
    flattened = flattened[:, : height * (length + height)]
    return flattened.reshape(leading, height, length + height)


def pair_bias(pair_counts, pair_in, pair_shift, pair_out):
    log_counts = jnp.log(1.0 + pair_counts.astype(jnp.float32))
    per_head = []
    for head_index in range(HEADS):
        summed = jnp.zeros(log_counts.shape, jnp.float32)
        for hidden_unit in range(PAIR_HIDDEN):
            inner = (
                pair_in[head_index, hidden_unit] * log_counts + pair_shift[head_index, hidden_unit]
            )
            summed = summed + pair_out[head_index, hidden_unit] * jax.nn.silu(inner)
        per_head.append(summed)
    return jnp.stack(per_head, 0)


def shards(bin_states, contacts, w_query, w_keyval, pair_in, pair_shift, pair_out, w_out):
    head_cols = HEADS * HEAD_DIM
    queries = jnp.dot(bin_states, w_query, preferred_element_type=jnp.float32).astype(jnp.bfloat16)
    key_values = jnp.dot(bin_states, w_keyval, preferred_element_type=jnp.float32).astype(
        jnp.bfloat16
    )
    query_block, keyval_block = (
        lax.all_gather(queries, "ka", axis=0, tiled=True),
        lax.all_gather(key_values, "ka", axis=0, tiled=True),
    )
    pb_count = lax.axis_size("pb")
    ka_count = lax.axis_size("ka")
    pb_index = lax.axis_index("pb")
    ka_index = lax.axis_index("ka")
    query_rows = query_block.shape[0]
    offsets = contacts.shape[1]
    span_ratio = offsets // query_rows
    lead_blocks = HALF_BAND // query_rows
    seq_len = query_rows * pb_count
    key_start = pb_index * query_rows + ka_index * offsets - HALF_BAND
    pieces = []
    for step_index in range(span_ratio + 1):
        amount = (lead_blocks - step_index) % pb_count
        if amount == 0:
            pieces.append(keyval_block)
        else:
            pieces.append(shifted(keyval_block, "pb", amount))
    key_window = jnp.concatenate(pieces, 0)
    for bit_pos in range(ka_count.bit_length() - 1):
        amount = -(span_ratio << bit_pos) % pb_count
        if amount != 0:
            arrived = shifted(key_window, "pb", amount)
            key_window = jnp.where(ka_index >> bit_pos & 1 == 1, arrived, key_window)
    sub_rows = min(512, query_rows)
    sub_count = query_rows // sub_rows
    key_span = sub_rows + offsets
    inv_root = 1.0 / HEAD_DIM**0.5
    row_pos = jnp.arange(sub_rows, dtype=jnp.int32)[:, None]
    col_pos = jnp.arange(key_span, dtype=jnp.int32)[None, :]

    def score_block(block_index):
        first_row = block_index * sub_rows
        rows_query = query_block.reshape(sub_rows, HEADS, HEAD_DIM)
        keys_here = key_window[:, :head_cols]
        key_heads = keys_here.reshape(key_span, HEADS, HEAD_DIM)
        bias_tile = shear_rows(pair_bias(contacts, pair_in, pair_shift, pair_out))
        scores = (
            jnp.einsum("ihd,khd->hik", rows_query, key_heads, preferred_element_type=jnp.float32)
            * inv_root
            + bias_tile
        )
        key_pos = key_start + first_row + col_pos
        allowed = (
            (col_pos >= row_pos)
            & (col_pos < row_pos + offsets)
            & (key_pos >= 0)
            & (key_pos < seq_len)
        )
        return jnp.where(allowed[None], scores, -1e30)

    block_ids = jnp.arange(sub_count, dtype=jnp.int32)
    scores = lax.map(score_block, block_ids)
    row_top = lax.pmax(jnp.max(scores, axis=3), "ka")

    def weigh_block(operands):
        block_scores, block_top, block_index = operands
        weights = jnp.exp(block_scores - block_top[:, :, None]).astype(jnp.bfloat16)
        totals = jnp.sum(weights, axis=2, dtype=jnp.float32)
        values_here = key_window[:, head_cols:]
        value_heads = values_here.reshape(key_span, HEADS, HEAD_DIM)
        numerators = jnp.einsum(
            "hik,khd->ihd", weights, value_heads, preferred_element_type=jnp.float32
        )
        return (numerators.reshape(sub_rows, head_cols), jnp.transpose(totals))

    numerators, totals = lax.map(weigh_block, (scores, row_top, block_ids))
    numerators = numerators.reshape(query_rows, head_cols)
    totals = totals.reshape(query_rows, HEADS)
    share_rows = query_rows // ka_count
    summed_num, summed_tot = lax.psum((numerators, totals), "ka")
    first_share = ka_index * share_rows
    summed_num = lax.dynamic_slice_in_dim(summed_num, first_share, share_rows, 0)
    summed_tot = lax.dynamic_slice_in_dim(summed_tot, first_share, share_rows, 0)
    attended = summed_num.reshape(share_rows, HEADS, HEAD_DIM) / summed_tot[:, :, None]
    attended = attended.reshape(share_rows, head_cols).astype(jnp.bfloat16)
    return jnp.dot(attended, w_out, preferred_element_type=jnp.float32).astype(jnp.bfloat16)


def solution(mesh):
    placed = (P(("pb", "ka"), None), P("pb", "ka"), P(), P(), P(), P(), P(), P())
    return jax.shard_map(
        shards, mesh=mesh, in_specs=placed, out_specs=P(("pb", "ka"), None), check_vma=False
    )
```

profile of v0, /device:TPU:0, one launch (start us, length us, event | category | flops | bytes accessed | tf_op | source)
XLA Modules:
  0.0 525.7 jit_solution(3791947021305828865)
XLA Ops:
  6.5 1.4 copy-done
  7.9 1.5 convolution_convert_fusion.1
  9.4 31.4 %all_gather.6 = bf16[512,512]{1,0:T(8,128)(2,1)S(1)} all-gather(bf16[64,512]{1,0:T(8,128)(2,1)S(1)} %convolution_convert_fusion.1), channel_id=1, replica_groups=mesh['pb'=16,'ka'=8] {'ka'}, dimensions={0}, use_global_device_ids=true | all-gather | bytes 589824 | tf_op jit(solution)/shard_map/all_gather | solution.py:48
  40.9 5.4 %collective-permute-start.1 = (bf16[512,512]{1,0:T(8,128)(2,1)S(1)}, bf16[512,512]{1,0:T(8,128)(2,1)S(1)}, u32[]{:S(2)}, u32[]{:S(2)}) collective-permute-start(bf16[512,512]{1,0:T(8,128)(2,1)S(1)} %all_gather.6), channel_id=1, source_target_pairs={{16,0},{24,8},{32,16},{40,24},{48,32},{56,40},{64,48},{72,56},{80,... | collective-permute-start | bytes 1572872 | tf_op jit(solution)/shard_map/ppermute | solution.py:15
  47.3 2.1 fusion.14
  49.4 2.1 fusion.17
  51.5 2.1 fusion.13
  53.5 2.1 fusion.16
  55.6 2.1 fusion.12
  57.7 2.1 fusion.15
  59.8 1.6 fusion.23
  61.5 1.6 fusion.22
  63.1 1.6 fusion.21
  70.2 3.0 collective-permute-start.4
  73.2 113.2 %add_bitcast_fusion = f32[1,512,2048]{2,1,0:T(8,128)} fusion(s32[512,2048]{1,0:T(8,128)S(1)} %copy-done.9, f32[]{:T(128)} %bitcast.193, f32[]{:T(128)} %bitcast.192, f32[]{:T(128)} %bitcast.191, f32[]{:T(128)} %bitcast.190, f32[]{:T(128)} %bitcast.189, f32[]{:T(128)} %bitcast.188, f32[]{:T(128)} %bitcast.187, f32[]{:T(128)} %bitcast.186, f32[]{:T(128)} %bitcast.185, ...), kind=kLoop, calls=%fused_computation.11 | loop fusion | flops 269484032 | bytes 8388992 | tf_op jit(solution)/shard_map/while/body/eval_jaxpr/stack | solution.py:37
  188.5 3.6 broadcast_select_fusion
  192.7 112.8 %add_bitcast_fusion.1 = f32[1,512,2048]{2,1,0:T(8,128)} fusion(s32[512,2048]{1,0:T(8,128)S(1)} %copy-done.10, f32[]{:T(128)} %bitcast.96, f32[]{:T(128)} %bitcast.95, f32[]{:T(128)} %bitcast.94, f32[]{:T(128)} %bitcast.93, f32[]{:T(128)} %bitcast.92, f32[]{:T(128)} %bitcast.91, f32[]{:T(128)} %bitcast.90, f32[]{:T(128)} %bitcast.89, f32[]{:T(128)} %bitcast.88, ...), kind=kLoop, calls=%fused_computation.12 | loop fusion | flops 269484032 | bytes 8388992 | tf_op jit(solution)/shard_map/while/body/eval_jaxpr/stack | solution.py:37
  305.5 8.5 %select_maximum_fusion = f32[2,512,2561]{2,1,0:T(8,128)} fusion(f32[1,512,2048]{2,1,0:T(8,128)} %add_bitcast_fusion, f32[1,512,2048]{2,1,0:T(8,128)} %add_bitcast_fusion.1), kind=kLoop, calls=%fused_computation | loop fusion | flops 10489856 | bytes 18878464 | tf_op jit(solution)/shard_map/while/body/eval_jaxpr/stack | solution.py:37
  314.1 15.9 %reshape.122 = f32[2622464]{0:T(1024)} reshape(f32[2,512,2561]{2,1,0:T(8,128)} %select_maximum_fusion) | data formatting | bytes 20979712
  330.0 16.6 %reshape.118 = f32[2,1311232]{1,0:T(2,128)} reshape(f32[2622464]{0:T(1024)} %reshape.122) | data formatting | bytes 20979712 | tf_op jit(solution)/shard_map/while/body/eval_jaxpr/reshape | solution.py:21
  346.6 8.5 %slice.977 = f32[2,1310720]{1,0:T(2,128)} slice(f32[2,1311232]{1,0:T(2,128)} %reshape.118), slice={[0:2], [0:1310720]} | slice | bytes 20971520 | tf_op jit(solution)/shard_map/while/body/eval_jaxpr/slice | solution.py:22
  355.4 29.0 %all_gather.7 = bf16[512,256]{1,0:T(8,128)(2,1)S(1)} all-gather(bf16[64,256]{1,0:T(8,128)(2,1)S(1)} %convolution_convert_fusion.2), channel_id=1, replica_groups=mesh['pb'=16,'ka'=8] {'ka'}, dimensions={0}, use_global_device_ids=true | all-gather | bytes 294912 | tf_op jit(solution)/shard_map/all_gather | solution.py:47
  384.4 1.3 fusion.3
  385.7 2.0 broadcast_select_fusion.1
  387.8 1.4 slice_bitcast_fusion
  389.1 1.6 copy.15
  390.7 10.8 %fusion.24 = (f32[2,512]{1,0:T(2,128)S(1)}, f32[2,512,2560]{2,1,0:T(8,128)}) fusion(f32[1,2,512,2560]{3,1,2,0:T(2,128)} %bitcast.233, bf16[320,2,8,128]{3,2,1,0:T(8,128)(2,1)} %get-tuple-element.31, pred[512,2560]{1,0:T(8,128)(4,1)S(1)} %fusion.3, bf16[512,256]{1,0:T(8,128)(2,1)S(1)} %all_gather.7), kind=kOutput, calls=%fused_computation.49 | convolution fusion | flops 681573376 | bytes 23859200 | tf_op jit(solution)/shard_map/while/body/eval_jaxpr/ihd,khd->hik/dot_general | solution.py:87
  401.5 18.0 %pmax.7 = f32[2,512]{1,0:T(2,128)S(1)} all-reduce(f32[2,512]{1,0:T(2,128)S(1)} %get-tuple-element.250), channel_id=1, replica_groups=mesh['pb'=16,'ka'=8] {'ka'}, use_global_device_ids=true, to_apply=%region_1.2 | all-reduce | flops 1024 | bytes 8192 | tf_op jit(solution)/shard_map/pmax | solution.py:102
  419.5 6.7 %fusion.4 = f32[2,128,512]{2,1,0:T(8,128)} fusion(bf16[2560,2,128]{0,2,1:T(8,128)(2,1)S(1)} %bitcast.234, f32[2,512,2560]{2,1,0:T(8,128)} %get-tuple-element.251, f32[2,512]{1,0:T(2,128)S(1)} %pmax.7), kind=kOutput, calls=%fused_computation.17 | convolution fusion | flops 676331520 | bytes 12324864 | tf_op jit(solution)/shard_map/while/body/eval_jaxpr/hik,khd->ihd/dot_general | solution.py:110
  426.3 5.6 %convert_reduce_fusion = f32[2,512]{1,0:T(2,128)S(1)} fusion(f32[2,512,2560]{2,1,0:T(8,128)} %get-tuple-element.251, f32[2,512]{1,0:T(2,128)S(1)} %pmax.7), kind=kLoop, calls=%fused_computation.4 | loop fusion | flops 10484736 | bytes 10493952 | tf_op jit(solution)/shard_map/while/body/eval_jaxpr/reduce_sum | solution.py:107
  431.9 16.1 %psum.15 = f32[512,2]{0,1:T(2,128)S(1)} all-reduce(f32[512,2]{0,1:T(2,128)S(1)} %bitcast.236), channel_id=1, replica_groups=mesh['pb'=16,'ka'=8] {'ka'}, use_global_device_ids=true, to_apply=%region_4.5 | all-reduce | flops 1024 | bytes 8192 | tf_op jit(solution)/shard_map/psum | solution.py:119
  448.1 68.8 %all-reduce.3.cloned.1.call-done = f32[512,256]{0,1:T(8,128)} async-done(((f32[512,256]{0,1:T(8,128)}), f32[512,256]{0,1:T(8,128)}) %all-reduce.3.cloned.1.call-update) | async-done | bytes 524304 | tf_op jit(solution)/shard_map/psum | solution.py:119
  (47 shorter events, 11.7 us)
Async XLA Ops:
  6.5 1.4 copy-start
  6.5 510.3 %all-reduce.3.cloned.1.call-start = ((), (), s32[]{:S(2)}) async-start(), calls=%async_computation | async-start | bytes 1048576 | tf_op jit(solution)/shard_map/psum | solution.py:119
  7.9 65.2 %copy-start.9 = (s32[512,2048]{1,0:T(8,128)S(1)}, s32[512,2048]{1,0:T(8,128)}, u32[]{:S(2)}) copy-start(s32[512,2048]{1,0:T(8,128)} %param.9) | copy-start | bytes 12582916
  40.8 24.7 %collective-permute-start = (bf16[512,512]{1,0:T(8,128)(2,1)S(1)}, bf16[512,512]{1,0:T(8,128)(2,1)S(1)}, u32[]{:S(2)}, u32[]{:S(2)}) collective-permute-start(bf16[512,512]{1,0:T(8,128)(2,1)S(1)} %all_gather.6), channel_id=1, source_target_pairs={{8,0},{16,8},{24,16},{32,24},{40,32},{48,40},{56,48},{64,56},{72,6... | collective-permute-start | bytes 1572872 | tf_op jit(solution)/shard_map/ppermute | solution.py:15
  40.9 26.8 %collective-permute-start.1 = (bf16[512,512]{1,0:T(8,128)(2,1)S(1)}, bf16[512,512]{1,0:T(8,128)(2,1)S(1)}, u32[]{:S(2)}, u32[]{:S(2)}) collective-permute-start(bf16[512,512]{1,0:T(8,128)(2,1)S(1)} %all_gather.6), channel_id=1, source_target_pairs={{16,0},{24,8},{32,16},{40,24},{48,32},{56,40},{64,48},{72,56},{80,... | collective-permute-start | bytes 1572872 | tf_op jit(solution)/shard_map/ppermute | solution.py:15
  46.2 22.3 %collective-permute-start.2 = (bf16[512,512]{1,0:T(8,128)(2,1)S(1)}, bf16[512,512]{1,0:T(8,128)(2,1)S(1)}, u32[]{:S(2)}, u32[]{:S(2)}) collective-permute-start(bf16[512,512]{1,0:T(8,128)(2,1)S(1)} %all_gather.6), channel_id=1, source_target_pairs={{24,0},{32,8},{40,16},{48,24},{56,32},{64,40},{72,48},{80,56},{88,... | collective-permute-start | bytes 1572872 | tf_op jit(solution)/shard_map/ppermute | solution.py:15
  46.8 22.5 %collective-permute-start.3 = (bf16[512,512]{1,0:T(8,128)(2,1)S(1)}, bf16[512,512]{1,0:T(8,128)(2,1)S(1)}, u32[]{:S(2)}, u32[]{:S(2)}) collective-permute-start(bf16[512,512]{1,0:T(8,128)(2,1)S(1)} %all_gather.6), channel_id=1, source_target_pairs={{32,0},{40,8},{48,16},{56,24},{64,32},{72,40},{80,48},{88,56},{96,... | collective-permute-start | bytes 1572872 | tf_op jit(solution)/shard_map/ppermute | solution.py:15
  70.2 118.4 %collective-permute-start.4 = (bf16[2560,512]{1,0:T(8,128)(2,1)}, bf16[2560,512]{1,0:T(8,128)(2,1)}, u32[]{:S(2)}, u32[]{:S(2)}) collective-permute-start(bf16[2560,512]{1,0:T(8,128)(2,1)} %constant_dynamic-update-slice_fusion), channel_id=1, source_target_pairs={{32,0},{40,8},{48,16},{56,24},{64,32},{72,40},{80,48},{88,56},{96,... | collective-permute-start | bytes 7864328 | tf_op jit(solution)/shard_map/ppermute | solution.py:15
  73.2 113.2 %copy-start.3 = (f32[2,32]{1,0:T(2,128)S(1)}, f32[2,32]{1,0:T(2,128)}, u32[]{:S(2)}) copy-start(f32[2,32]{1,0:T(2,128)} %param.13) | copy-start | bytes 772
  73.2 113.9 %copy-start.4 = (f32[2,32]{1,0:T(2,128)S(1)}, f32[2,32]{1,0:T(2,128)}, u32[]{:S(2)}) copy-start(f32[2,32]{1,0:T(2,128)} %param.12) | copy-start | bytes 772
  73.2 114.6 %copy-start.5 = (f32[2,32]{1,0:T(2,128)S(1)}, f32[2,32]{1,0:T(2,128)}, u32[]{:S(2)}) copy-start(f32[2,32]{1,0:T(2,128)} %param.14) | copy-start | bytes 772
  186.3 6.4 %copy-start.10 = (s32[512,2048]{1,0:T(8,128)S(1)}, s32[512,2048]{1,0:T(8,128)}, u32[]{:S(2)}) copy-start(s32[512,2048]{1,0:T(8,128)} %param.9) | copy-start | bytes 12582916
  192.1 193.6 %collective-permute-start.5 = (bf16[2560,512]{1,0:T(8,128)(2,1)}, bf16[2560,512]{1,0:T(8,128)(2,1)}, u32[]{:S(2)}, u32[]{:S(2)}) collective-permute-start(bf16[2560,512]{1,0:T(8,128)(2,1)} %broadcast_select_fusion), channel_id=1, source_target_pairs={{64,0},{72,8},{80,16},{88,24},{96,32},{104,40},{112,48},{120,56},{... | collective-permute-start | bytes 7864328 | tf_op jit(solution)/shard_map/ppermute | solution.py:15
  346.6 8.6 %copy-start.7 = (bf16[1536,256]{1,0:T(8,128)(2,1)S(1)}, bf16[1536,256]{1,0:T(8,128)(2,1)}, u32[]{:S(2)}) copy-start(bf16[1536,256]{1,0:T(8,128)(2,1)} %param.10) | copy-start | bytes 2359300
  346.6 8.6 %copy-start.8 = (bf16[64,1536]{1,0:T(8,128)(2,1)S(1)}, bf16[64,1536]{1,0:T(8,128)(2,1)}, u32[]{:S(2)}) copy-start(bf16[64,1536]{1,0:T(8,128)(2,1)} %param.8) | copy-start | bytes 589828
  390.7 28.8 %copy-start.2 = (bf16[2560,256]{0,1:T(8,128)(2,1)S(1)}, bf16[2560,256]{0,1:T(8,128)(2,1)}, u32[]{:S(2)}) copy-start(bf16[2560,256]{0,1:T(8,128)(2,1)} %copy.15) | copy-start | bytes 3932164
  426.3 91.6 %copy-start.6 = (bf16[256,1536]{1,0:T(8,128)(2,1)S(1)}, bf16[256,1536]{1,0:T(8,128)(2,1)}, u32[]{:S(2)}) copy-start(bf16[256,1536]{1,0:T(8,128)(2,1)} %param.15) | copy-start | bytes 2359300
  426.3 92.6 %copy-start.1 = (bf16[1536,512]{1,0:T(8,128)(2,1)S(1)}, bf16[1536,512]{1,0:T(8,128)(2,1)}, u32[]{:S(2)}) copy-start(bf16[1536,512]{1,0:T(8,128)(2,1)} %param.11) | copy-start | bytes 4718596
Sparse Core Ops, SparseCore 0:
  426.4 90.4 all-reduce.2
where the time goes:
time: 528 us; the launch traced here: 526 us
  other arithmetic  248 us (47%)
  blocking collectives  94.5 us (18%)
  waiting for transfers between devices  70.1 us (13%)
  local copies, waits for them, and re-layouts  69.3 us (13%)
  matrix products  20.2 us (4%)
  between operations  13.5 us (3%)
  starting transfers between devices  10 us (2%)
    another operation x3, other arithmetic, pair_bias(): return jnp.stack(per_head, 0)  234 us
    psum x1, waiting for transfers between devices, shards(): summed_num, summed_tot = lax.psum((numerators, totals), 'ka')  68.8 us
    all_gather x1, blocking collectives, shards(): lax.all_gather(key_values, 'ka', axis=0, tiled=True)  31.4 us
    all_gather x1, blocking collectives, shards(): lax.all_gather(queries, 'ka', axis=0, tiled=True)  29 us
    unnamed x28, local copies, waits for them, and re-layouts  22.1 us
    pmax x1, blocking collectives, shards(): row_top = lax.pmax(jnp.max(scores, axis=3), 'ka')  18 us
    reshape x1, local copies, waits for them, and re-layouts, shear_rows(): flattened = padded.reshape(leading, height * (length + height + 1))  16.6 us
    psum x1, blocking collectives, shards(): summed_num, summed_tot = lax.psum((numerators, totals), 'ka')  16.1 us
  transfers between devices with their start and end apart: 7, of which 2 were waited for; matrix products, arithmetic and copies ran while one was open for 58% of the time, Pallas kernels for 0%

commit v1 on v0

--- a/solution.py
+++ b/solution.py
@@ -7,6 +7,13 @@
 HEAD_DIM = 128
 PAIR_HIDDEN = 32
 HALF_BAND = 8192
+
+
+def exchange_gather(array, mesh_axis, dim):
+    size = lax.axis_size(mesh_axis)
+    shards = jnp.stack([array for _ in range(size)])
+    shards = lax.all_to_all(shards, mesh_axis, split_axis=0, concat_axis=0)
+    return jnp.concatenate(shards, axis=dim)
 
 
 def shifted(block, axis, distance):
@@ -44,7 +51,7 @@
         jnp.bfloat16
     )
     query_block, keyval_block = (
-        lax.all_gather(queries, "ka", axis=0, tiled=True),
+        exchange_gather(queries, "ka", 0),
         lax.all_gather(key_values, "ka", axis=0, tiled=True),
     )
     pb_count = lax.axis_size("pb")

time: 528 us -> 499 us (0.945)
  blocking collectives: 94.5 us -> 66.5 us
  local copies, waits for them, and re-layouts: 69.3 us -> 59 us
    all_gather x1 -> x0, blocking collectives: 29 us -> none  [shards(): lax.all_gather(queries, 'ka', axis=0, tiled=True)]
    unnamed x28 -> x24, local copies, waits for them, and re-layouts: 22.1 us -> 22.1 us
  transfers between devices with their start and end apart: 7 -> 8, of which waited for: 2 -> 2; matrix products, arithmetic and copies ran while one was open for 58% -> 61% of each run, Pallas kernels for 0% -> 0%
where the time goes in v1:
time: 499 us; the launch traced here: 497 us
  other arithmetic  248 us (50%)
  waiting for transfers between devices  73.9 us (15%)
  blocking collectives  66.5 us (13%)
  local copies, waits for them, and re-layouts  59 us (12%)
  matrix products  21.3 us (4%)
  starting transfers between devices  14.2 us (3%)
  between operations  13.5 us (3%)
    another operation x3, other arithmetic, pair_bias(): return jnp.stack(per_head, 0)  234 us
    psum x1, waiting for transfers between devices, shards(): summed_num, summed_tot = lax.psum((numerators, totals), 'ka')  68 us
    all_gather x1, blocking collectives, shards(): lax.all_gather(key_values, 'ka', axis=0, tiled=True)  31.4 us
    unnamed x24, local copies, waits for them, and re-layouts  22.1 us
    pmax x1, blocking collectives, shards(): row_top = lax.pmax(jnp.max(scores, axis=3), 'ka')  19.1 us
    reshape x1, local copies, waits for them, and re-layouts, shear_rows(): flattened = padded.reshape(leading, height * (length + height + 1))  16.6 us
    psum x1, blocking collectives, shards(): summed_num, summed_tot = lax.psum((numerators, totals), 'ka')  16 us
    dot_general x1, matrix products, score_block(): jnp.einsum('ihd,khd->hik', rows_query, key_heads, preferred_element_type=...  10.8 us
  transfers between devices with their start and end apart: 8, of which 2 were waited for; matrix products, arithmetic and copies ran while one was open for 61% of the time, Pallas kernels for 0%

profile of v1, /device:TPU:0, one launch (start us, length us, event | category | flops | bytes accessed | tf_op | source)
XLA Modules:
  0.0 496.5 jit_solution(14549392485045058470)
XLA Ops:
  6.5 1.4 copy-done
  7.9 1.3 convolution_convert_fusion.1
  9.3 31.4 %all_gather.3 = bf16[512,512]{1,0:T(8,128)(2,1)S(1)} all-gather(bf16[64,512]{1,0:T(8,128)(2,1)S(1)} %convolution_convert_fusion.1), channel_id=1, replica_groups=mesh['pb'=16,'ka'=8] {'ka'}, dimensions={0}, use_global_device_ids=true | all-gather | bytes 589824 | tf_op jit(solution)/shard_map/all_gather | solution.py:55
  40.7 5.4 %collective-permute-start.1 = (bf16[512,512]{1,0:T(8,128)(2,1)S(1)}, bf16[512,512]{1,0:T(8,128)(2,1)S(1)}, u32[]{:S(2)}, u32[]{:S(2)}) collective-permute-start(bf16[512,512]{1,0:T(8,128)(2,1)S(1)} %all_gather.3), channel_id=1, source_target_pairs={{16,0},{24,8},{32,16},{40,24},{48,32},{56,40},{64,48},{72,56},{80,... | collective-permute-start | bytes 1572872 | tf_op jit(solution)/shard_map/ppermute | solution.py:22
  47.1 1.5 convolution_convert_fusion.2
  49.3 4.1 all-to-all-start
  59.9 0.8 constant_dynamic-update-slice_fusion.4
  60.8 0.8 constant_dynamic-update-slice_fusion.3
  61.6 5.9 %collective-permute-done.1 = bf16[512,512]{1,0:T(8,128)(2,1)S(1)} collective-permute-done((bf16[512,512]{1,0:T(8,128)(2,1)S(1)}, bf16[512,512]{1,0:T(8,128)(2,1)S(1)}, u32[]{:S(2)}, u32[]{:S(2)}) %collective-permute-start.1) | collective-permute-done | bytes 524320 | tf_op jit(solution)/shard_map/ppermute | solution.py:22
  67.5 0.8 constant_dynamic-update-slice_fusion.2
  68.3 0.8 constant_dynamic-update-slice_fusion.1
  69.2 0.8 constant_dynamic-update-slice_fusion
  70.0 3.0 collective-permute-start.4
  73.0 113.1 %add_bitcast_fusion = f32[1,512,2048]{2,1,0:T(8,128)} fusion(s32[512,2048]{1,0:T(8,128)S(1)} %copy-done.7, f32[]{:T(128)} %bitcast.193, f32[]{:T(128)} %bitcast.192, f32[]{:T(128)} %bitcast.191, f32[]{:T(128)} %bitcast.190, f32[]{:T(128)} %bitcast.189, f32[]{:T(128)} %bitcast.188, f32[]{:T(128)} %bitcast.187, f32[]{:T(128)} %bitcast.186, f32[]{:T(128)} %bitcast.185, ...), kind=kLoop, calls=%fused_computation.11 | loop fusion | flops 269484032 | bytes 8388992 | tf_op jit(solution)/shard_map/while/body/eval_jaxpr/stack | solution.py:44
  188.3 3.6 broadcast_select_fusion
  192.5 112.8 %add_bitcast_fusion.1 = f32[1,512,2048]{2,1,0:T(8,128)} fusion(s32[512,2048]{1,0:T(8,128)S(1)} %copy-done.8, f32[]{:T(128)} %bitcast.96, f32[]{:T(128)} %bitcast.95, f32[]{:T(128)} %bitcast.94, f32[]{:T(128)} %bitcast.93, f32[]{:T(128)} %bitcast.92, f32[]{:T(128)} %bitcast.91, f32[]{:T(128)} %bitcast.90, f32[]{:T(128)} %bitcast.89, f32[]{:T(128)} %bitcast.88, ...), kind=kLoop, calls=%fused_computation.12 | loop fusion | flops 269484032 | bytes 8388992 | tf_op jit(solution)/shard_map/while/body/eval_jaxpr/stack | solution.py:44
  305.3 1.3 fusion.3
  306.7 8.5 %select_maximum_fusion = f32[2,512,2561]{2,1,0:T(8,128)} fusion(f32[1,512,2048]{2,1,0:T(8,128)} %add_bitcast_fusion, f32[1,512,2048]{2,1,0:T(8,128)} %add_bitcast_fusion.1), kind=kLoop, calls=%fused_computation | loop fusion | flops 10489856 | bytes 18878464 | tf_op jit(solution)/shard_map/while/body/eval_jaxpr/stack | solution.py:44
  315.2 15.9 %reshape.119 = f32[2622464]{0:T(1024)} reshape(f32[2,512,2561]{2,1,0:T(8,128)} %select_maximum_fusion) | data formatting | bytes 20979712
  331.1 16.6 %reshape.115 = f32[2,1311232]{1,0:T(2,128)} reshape(f32[2622464]{0:T(1024)} %reshape.119) | data formatting | bytes 20979712 | tf_op jit(solution)/shard_map/while/body/eval_jaxpr/reshape | solution.py:28
  347.7 8.4 %slice.977 = f32[2,1310720]{1,0:T(2,128)} slice(f32[2,1311232]{1,0:T(2,128)} %reshape.115), slice={[0:2], [0:1310720]} | slice | bytes 20971520 | tf_op jit(solution)/shard_map/while/body/eval_jaxpr/slice | solution.py:29
  356.3 2.0 broadcast_select_fusion.1
  358.3 1.4 slice_bitcast_fusion
  359.7 1.6 copy.14
  361.3 10.8 %fusion.23 = (f32[2,512]{1,0:T(2,128)S(1)}, f32[2,512,2560]{2,1,0:T(8,128)}) fusion(f32[1,2,512,2560]{3,1,2,0:T(2,128)} %bitcast.224, bf16[320,2,8,128]{3,2,1,0:T(8,128)(2,1)} %get-tuple-element.31, bf16[512,2,128]{2,1,0:T(2,128)(2,1)S(1)} %reshape_reshape.4, pred[512,2560]{1,0:T(8,128)(4,1)S(1)} %fusion.3), kind=kOutput, calls=%fused_computation.48 | convolution fusion | flops 681573376 | bytes 23859200 | tf_op jit(solution)/shard_map/while/body/eval_jaxpr/ihd,khd->hik/dot_general | solution.py:94
  372.1 19.1 %pmax.7 = f32[2,512]{1,0:T(2,128)S(1)} all-reduce(f32[2,512]{1,0:T(2,128)S(1)} %get-tuple-element.250), channel_id=1, replica_groups=mesh['pb'=16,'ka'=8] {'ka'}, use_global_device_ids=true, to_apply=%region_1.2 | all-reduce | flops 1024 | bytes 8192 | tf_op jit(solution)/shard_map/pmax | solution.py:109
  391.1 6.7 %fusion.4 = f32[2,128,512]{2,1,0:T(8,128)} fusion(bf16[2560,2,128]{0,2,1:T(8,128)(2,1)S(1)} %bitcast.225, f32[2,512,2560]{2,1,0:T(8,128)} %get-tuple-element.251, f32[2,512]{1,0:T(2,128)S(1)} %pmax.7), kind=kOutput, calls=%fused_computation.17 | convolution fusion | flops 676331520 | bytes 12324864 | tf_op jit(solution)/shard_map/while/body/eval_jaxpr/hik,khd->ihd/dot_general | solution.py:117
  397.9 5.6 %convert_reduce_fusion = f32[2,512]{1,0:T(2,128)S(1)} fusion(f32[2,512,2560]{2,1,0:T(8,128)} %get-tuple-element.251, f32[2,512]{1,0:T(2,128)S(1)} %pmax.7), kind=kLoop, calls=%fused_computation.4 | loop fusion | flops 10484736 | bytes 10493952 | tf_op jit(solution)/shard_map/while/body/eval_jaxpr/reduce_sum | solution.py:114
  403.6 16.0 %psum.15 = f32[512,2]{0,1:T(2,128)S(1)} all-reduce(f32[512,2]{0,1:T(2,128)S(1)} %bitcast.227), channel_id=1, replica_groups=mesh['pb'=16,'ka'=8] {'ka'}, use_global_device_ids=true, to_apply=%region_4.5 | all-reduce | flops 1024 | bytes 8192 | tf_op jit(solution)/shard_map/psum | solution.py:126
  419.7 68.0 %all-reduce.3.cloned.1.call-done = f32[512,256]{0,1:T(8,128)} async-done(((f32[512,256]{0,1:T(8,128)}), f32[512,256]{0,1:T(8,128)}) %all-reduce.3.cloned.1.call-update) | async-done | bytes 524304 | tf_op jit(solution)/shard_map/psum | solution.py:126
  487.7 1.0 fusion.8
  488.7 1.0 convolution_convert_fusion
  (46 shorter events, 11.2 us)
Async XLA Ops:
  6.5 1.4 copy-start
  6.5 46.9 %copy-start.3 = (f32[2,32]{1,0:T(2,128)S(1)}, f32[2,32]{1,0:T(2,128)}, u32[]{:S(2)}) copy-start(f32[2,32]{1,0:T(2,128)} %param.13) | copy-start | bytes 772
  6.5 48.4 %copy-start.4 = (f32[2,32]{1,0:T(2,128)S(1)}, f32[2,32]{1,0:T(2,128)}, u32[]{:S(2)}) copy-start(f32[2,32]{1,0:T(2,128)} %param.12) | copy-start | bytes 772
  6.5 49.9 %copy-start.5 = (f32[2,32]{1,0:T(2,128)S(1)}, f32[2,32]{1,0:T(2,128)}, u32[]{:S(2)}) copy-start(f32[2,32]{1,0:T(2,128)} %param.14) | copy-start | bytes 772
  40.7 20.1 %collective-permute-start = (bf16[512,512]{1,0:T(8,128)(2,1)S(1)}, bf16[512,512]{1,0:T(8,128)(2,1)S(1)}, u32[]{:S(2)}, u32[]{:S(2)}) collective-permute-start(bf16[512,512]{1,0:T(8,128)(2,1)S(1)} %all_gather.3), channel_id=1, source_target_pairs={{8,0},{16,8},{24,16},{32,24},{40,32},{48,40},{56,48},{64,56},{72,6... | collective-permute-start | bytes 1572872 | tf_op jit(solution)/shard_map/ppermute | solution.py:22
  40.7 26.8 %collective-permute-start.1 = (bf16[512,512]{1,0:T(8,128)(2,1)S(1)}, bf16[512,512]{1,0:T(8,128)(2,1)S(1)}, u32[]{:S(2)}, u32[]{:S(2)}) collective-permute-start(bf16[512,512]{1,0:T(8,128)(2,1)S(1)} %all_gather.3), channel_id=1, source_target_pairs={{16,0},{24,8},{32,16},{40,24},{48,32},{56,40},{64,48},{72,56},{80,... | collective-permute-start | bytes 1572872 | tf_op jit(solution)/shard_map/ppermute | solution.py:22
  46.1 22.2 %collective-permute-start.2 = (bf16[512,512]{1,0:T(8,128)(2,1)S(1)}, bf16[512,512]{1,0:T(8,128)(2,1)S(1)}, u32[]{:S(2)}, u32[]{:S(2)}) collective-permute-start(bf16[512,512]{1,0:T(8,128)(2,1)S(1)} %all_gather.3), channel_id=1, source_target_pairs={{24,0},{32,8},{40,16},{48,24},{56,32},{64,40},{72,48},{80,56},{88,... | collective-permute-start | bytes 1572872 | tf_op jit(solution)/shard_map/ppermute | solution.py:22
  46.7 22.5 %collective-permute-start.3 = (bf16[512,512]{1,0:T(8,128)(2,1)S(1)}, bf16[512,512]{1,0:T(8,128)(2,1)S(1)}, u32[]{:S(2)}, u32[]{:S(2)}) collective-permute-start(bf16[512,512]{1,0:T(8,128)(2,1)S(1)} %all_gather.3), channel_id=1, source_target_pairs={{32,0},{40,8},{48,16},{56,24},{64,32},{72,40},{80,48},{88,56},{96,... | collective-permute-start | bytes 1572872 | tf_op jit(solution)/shard_map/ppermute | solution.py:22
  49.3 306.9 %all-to-all-start = ((bf16[8,64,256]{2,1,0:T(8,128)(2,1)}), bf16[8,64,256]{2,1,0:T(8,128)(2,1)S(1)}, u32[]{:S(2)}, u32[]{:S(2)}) async-start(bf16[8,64,256]{2,1,0:T(8,128)(2,1)} %stack.11), calls=%async_computation | async-start | bytes 524288 | tf_op jit(solution)/shard_map/all_to_all | solution.py:15
  53.4 434.3 %all-reduce.3.cloned.1.call-start = ((), (), s32[]{:S(2)}) async-start(), calls=%async_computation.1 | async-start | bytes 1048576 | tf_op jit(solution)/shard_map/psum | solution.py:126
  53.5 19.5 %copy-start.7 = (s32[512,2048]{1,0:T(8,128)S(1)}, s32[512,2048]{1,0:T(8,128)}, u32[]{:S(2)}) copy-start(s32[512,2048]{1,0:T(8,128)} %param.9) | copy-start | bytes 12582916
  70.0 118.3 %collective-permute-start.4 = (bf16[2560,512]{1,0:T(8,128)(2,1)}, bf16[2560,512]{1,0:T(8,128)(2,1)}, u32[]{:S(2)}, u32[]{:S(2)}) collective-permute-start(bf16[2560,512]{1,0:T(8,128)(2,1)} %constant_dynamic-update-slice_fusion), channel_id=1, source_target_pairs={{32,0},{40,8},{48,16},{56,24},{64,32},{72,40},{80,48},{88,56},{96,... | collective-permute-start | bytes 7864328 | tf_op jit(solution)/shard_map/ppermute | solution.py:22
  186.1 6.4 %copy-start.8 = (s32[512,2048]{1,0:T(8,128)S(1)}, s32[512,2048]{1,0:T(8,128)}, u32[]{:S(2)}) copy-start(s32[512,2048]{1,0:T(8,128)} %param.9) | copy-start | bytes 12582916
  191.9 164.4 %collective-permute-start.5 = (bf16[2560,512]{1,0:T(8,128)(2,1)}, bf16[2560,512]{1,0:T(8,128)(2,1)}, u32[]{:S(2)}, u32[]{:S(2)}) collective-permute-start(bf16[2560,512]{1,0:T(8,128)(2,1)} %broadcast_select_fusion), channel_id=1, source_target_pairs={{64,0},{72,8},{80,16},{88,24},{96,32},{104,40},{112,48},{120,56},{... | collective-permute-start | bytes 7864328 | tf_op jit(solution)/shard_map/ppermute | solution.py:22
  361.3 29.9 %copy-start.2 = (bf16[2560,256]{0,1:T(8,128)(2,1)S(1)}, bf16[2560,256]{0,1:T(8,128)(2,1)}, u32[]{:S(2)}) copy-start(bf16[2560,256]{0,1:T(8,128)(2,1)} %copy.14) | copy-start | bytes 3932164
  397.9 90.8 %copy-start.6 = (bf16[256,1536]{1,0:T(8,128)(2,1)S(1)}, bf16[256,1536]{1,0:T(8,128)(2,1)}, u32[]{:S(2)}) copy-start(bf16[256,1536]{1,0:T(8,128)(2,1)} %param.15) | copy-start | bytes 2359300
  397.9 91.8 %copy-start.1 = (bf16[1536,512]{1,0:T(8,128)(2,1)S(1)}, bf16[1536,512]{1,0:T(8,128)(2,1)}, u32[]{:S(2)}) copy-start(bf16[1536,512]{1,0:T(8,128)(2,1)} %param.11) | copy-start | bytes 4718596
Sparse Core Ops, SparseCore 0:
  398.0 89.6 all-reduce.2
